TPU v7x, 256 devices: a whole 4x4x8 slice. The times are simulated.
256 devices in a mesh: px: 4 (over z_lo), py: 8 (over y, core), ch: 8 (over z_hi, x).
Axes of the slice: x: 4, y: 4, z: 8 (z_hi: 2, z_lo: 4; z = z_hi * 4 + z_lo), core: 2. Of those that a mesh axis runs over, the one named last changes fastest.
Arguments:
- features: bfloat16 [128, 12, 8, 4, 512], P('ch', None, 'py', 'px'), may hold values from -6 to 6
- cotangent: bfloat16 [128, 12, 8, 4, 512], P('ch', None, 'py', 'px'), may hold values from -6 to 6
- weight: bfloat16 [3, 3, 128, 128], replicated, may hold values from -0.1875 to 0.1875
- edge_table: int32 [12, 4, 3], replicated, may hold values from 0 to 11, as said below
- corner_table: int32 [12, 4, 2], replicated, may hold values from 0 to 11, as said below
Outputs:
- activation: bfloat16 [128, 12, 8, 4, 512], P('ch', None, 'py', 'px')
- input_grad: bfloat16 [128, 12, 8, 4, 512], P('ch', None, 'py', 'px')
Inputs may be any that keep to these rules, and one draw needn't show every extreme that they name: edge_table[f, e] = (g, s, r): beyond edge e of face f lie the pixels of side s of face g, in reverse order if r = 1; every side of every face is named exactly once, and if (f, e) names (g, s) then (g, s) names (f, e) with the same r. corner_table[f, c] = (h, q): corner c of face f takes corner pixel q of face h; in each corner column every face appears once, and each q appears 12 times.
All inputs are finite; a program needn't handle non-finite values.
Results may differ from a plain program's by a relative error of at most 0.0049.
Values may be sent and summed in bfloat16 or wider, within the bound.
A program may use at most 192 MiB of HBM per device.

v0:
```python
import jax
import jax.numpy as jnp
from jax import lax
from jax.sharding import PartitionSpec as P

RB = 32


def with_halo(array, sides, width):
    for axis, dim in sides:
        size, length = (lax.axis_size(axis), array.shape[dim])
        up = [(i, (i + 1) % size) for i in range(size - 1)]
        down = [(j, i) for i, j in up]
        last = lax.slice_in_dim(array, length - width, length, axis=dim)
        leading = lax.slice_in_dim(array, 0, width, axis=dim)
        before = lax.ppermute(last, axis, up)
        after = lax.ppermute(leading, axis, down)
        array = jnp.concatenate([before, array, after], axis=dim)
    return array


def edge_strips(lines, edge_table, corner_table):
    chan_count = lines.shape[0]
    face_count = lines.shape[1]
    side_len = lines.shape[3]
    flat_lines = lines.reshape(chan_count, face_count * 4, side_len)
    pixels = jnp.stack(
        [lines[:, :, 0, 0], lines[:, :, 0, -1], lines[:, :, 1, 0], lines[:, :, 1, -1]], axis=2
    ).reshape(chan_count, face_count * 4)
    corner_index = corner_table[:, :, 0] * 4 + corner_table[:, :, 1]
    corner_vals = jnp.take(pixels, corner_index, axis=1)
    strips = []
    for edge_num, start_corner, end_corner in ((0, 0, 1), (1, 2, 3), (2, 0, 2), (3, 1, 3)):
        source_row = edge_table[:, edge_num, 0] * 4 + edge_table[:, edge_num, 1]
        strip_line = jnp.take(flat_lines, source_row, axis=1)
        flipped = (edge_table[:, edge_num, 2] == 1)[None, :, None]
        strip_line = jnp.where(flipped, strip_line[:, :, ::-1], strip_line)
        strips.append(
            jnp.concatenate(
                [
                    corner_vals[:, :, start_corner : start_corner + 1],
                    strip_line,
                    corner_vals[:, :, end_corner : end_corner + 1],
                ],
                axis=2,
            )
        )
    return strips


def face_lines_of(field, row_pos, col_pos, px_count, py_count):
    chan_block = field.shape[0]
    face_count = field.shape[1]
    col_len = field.shape[2]
    row_len = field.shape[3]
    side_len = row_len * px_count
    blank = jnp.zeros((chan_block, face_count, side_len), jnp.float32)

    def placed(values, offset, active):
        return jnp.where(
            active,
            lax.dynamic_update_slice_in_dim(blank, values.astype(jnp.float32), offset, 2),
            0.0,
        )

    contrib = jnp.stack(
        [
            placed(field[:, :, 0, :], row_pos * row_len, col_pos == 0),
            placed(field[:, :, -1, :], row_pos * row_len, col_pos == py_count - 1),
            placed(field[:, :, :, 0], col_pos * col_len, row_pos == 0),
            placed(field[:, :, :, -1], col_pos * col_len, row_pos == px_count - 1),
        ],
        axis=2,
    )
    return lax.psum(contrib.astype(jnp.bfloat16), ("px", "py"))


def pad_field(field, edge_table, corner_table):
    col_len = field.shape[2]
    row_len = field.shape[3]
    row_pos = lax.axis_index("px")
    col_pos = lax.axis_index("py")
    px_count = lax.axis_size("px")
    py_count = lax.axis_size("py")
    padded = with_halo(field, (("px", 3), ("py", 2)), 1)
    lines = face_lines_of(field, row_pos, col_pos, px_count, py_count)
    strips = edge_strips(lines, edge_table, corner_table)
    top_row = lax.dynamic_slice_in_dim(strips[0], row_pos * row_len, row_len + 2, 2)
    bottom_row = lax.dynamic_slice_in_dim(strips[1], row_pos * row_len, row_len + 2, 2)
    left_col = lax.dynamic_slice_in_dim(strips[2], col_pos * col_len, col_len + 2, 2)
    right_col = lax.dynamic_slice_in_dim(strips[3], col_pos * col_len, col_len + 2, 2)
    padded = padded.at[:, :, 0, :].set(jnp.where(col_pos == 0, top_row, padded[:, :, 0, :]))
    padded = padded.at[:, :, -1, :].set(
        jnp.where(col_pos == py_count - 1, bottom_row, padded[:, :, -1, :])
    )
    padded = padded.at[:, :, :, 0].set(jnp.where(row_pos == 0, left_col, padded[:, :, :, 0]))
    padded = padded.at[:, :, :, -1].set(
        jnp.where(row_pos == px_count - 1, right_col, padded[:, :, :, -1])
    )
    return padded


def forward_taps(padded, taps, out_cols, out_rows):
    summed = None
    for tap_row in range(3):
        for tap_col in range(3):
            window = padded[:, :, tap_row : tap_row + out_cols, tap_col : tap_col + out_rows]
            term_val = jnp.einsum(
                "oc,cfab->ofab", taps[tap_row, tap_col], window, preferred_element_type=jnp.float32
            )
            summed = term_val if summed is None else summed + term_val
    return summed


def backward_taps(padded, taps, out_cols, out_rows):
    summed = None
    for tap_row in range(3):
        for tap_col in range(3):
            window = padded[
                :, :, 2 - tap_row : 2 - tap_row + out_cols, 2 - tap_col : 2 - tap_col + out_rows
            ]
            term_val = jnp.einsum(
                "oc,ofab->cfab", taps[tap_row, tap_col], window, preferred_element_type=jnp.float32
            )
            summed = term_val if summed is None else summed + term_val
    return summed


def gate_outputs(preact, cotangent):
    sigmoid_val = jax.nn.sigmoid(preact)
    activation = (preact * sigmoid_val).astype(jnp.bfloat16)
    gated = (
        cotangent.astype(jnp.float32) * sigmoid_val * (1.0 + preact * (1.0 - sigmoid_val))
    ).astype(jnp.bfloat16)
    return (activation, gated)


def local(features, cotangent, weight, edge_table, corner_table):
    chan_block = features.shape[0]
    face_count = features.shape[1]
    tile_len = features.shape[4]
    row_len = RB
    col_len = tile_len // row_len
    features = features.reshape(chan_block, face_count, col_len, row_len)
    cotangent = cotangent.reshape(chan_block, face_count, col_len, row_len)
    ch_pos = lax.axis_index("ch")
    feat_pad = pad_field(features, edge_table, corner_table)
    own_taps = lax.dynamic_slice_in_dim(weight, ch_pos * chan_block, chan_block, 2)
    piece_taps = own_taps
    preact = forward_taps(
        lax.all_gather(feat_pad, "ch", axis=0, tiled=True), piece_taps, col_len, row_len
    )
    activation, gated = gate_outputs(preact, cotangent)
    grad_pad = pad_field(gated, edge_table, corner_table)
    input_taps = lax.dynamic_slice_in_dim(weight, ch_pos * chan_block, chan_block, 3)
    piece_taps = input_taps
    input_grad = backward_taps(
        lax.all_gather(grad_pad, "ch", axis=0, tiled=True), piece_taps, col_len, row_len
    ).astype(jnp.bfloat16)
    out_shape = (chan_block, face_count, 1, 1, tile_len)
    return (activation.reshape(out_shape), input_grad.reshape(out_shape))


def solution(mesh):
    return jax.shard_map(
        local,
        mesh=mesh,
        in_specs=(P("ch", None, "py", "px", None), P("ch", None, "py", "px", None), P(), P(), P()),
        out_specs=(P("ch", None, "py", "px", None), P("ch", None, "py", "px", None)),
        check_vma=False,
    )
```

profile of v0, /device:TPU:8, one launch (start us, length us, event | category | flops | bytes accessed | tf_op | source)
XLA Modules:
  0.0 1055.1 jit_solution(10775510683861696942)
XLA Ops:
  11.2 3.0 copy.696
  16.1 2.7 select_n.196
  18.7 2.7 select_n.200
  23.1 2.6 copy.698
  27.0 7.1 collective-permute-start
  43.6 1.9 collective-permute-start.2
  45.5 3.9 collective-permute-start.3
  53.1 254.8 %all-reduce.3.cloned.1.call-done = bf16[16,12,4,128]{1,0,3,2:T(8,128)(2,1)} async-done(((bf16[16,12,4,128]{1,0,3,2:T(8,128)(2,1)}), bf16[16,12,4,128]{1,0,3,2:T(8,128)(2,1)}) %all-reduce.3.cloned.1.call-update) | async-done | bytes 196624 | tf_op jit(solution)/shard_map/psum | solution.py:75
  307.9 3.0 copy.702
  318.9 3.8 scatter.30
  326.8 18.3 %scatter.31 = bf16[16,12,18,34]{3,0,2,1:T(8,128)(2,1)S(1)} dynamic-update-slice(bf16[16,12,18,34]{3,0,2,1:T(8,128)(2,1)S(1)} %scatter.30, bf16[16,12,18,1]{3,0,2,1:T(8,128)(2,1)S(1)} %copy.707, s32[]{:T(128)} %constant.235.clone.1, s32[]{:T(128)} %constant.235.clone.1, s32[]{:T(128)} %constant.235.clone.1, s32[]{:T(128)} %constant.249.clone.1) | dynamic-update-slice | bytes 13828 | tf_op jit(solution)/shard_map/scatter | solution.py:97
  347.9 162.8 %all-gather.3.cloned.1.call-done = bf16[128,12,18,34]{3,0,2,1:T(8,128)(2,1)} async-done(((bf16[16,12,18,34]{3,0,2,1:T(8,128)(2,1)}), bf16[128,12,18,34]{3,0,2,1:T(8,128)(2,1)}) %all-gather.3.cloned.1.call-update) | async-done | bytes 1880080 | tf_op jit(solution)/shard_map/all_gather | solution.py:151
  510.7 4.7 fusion.20
  524.6 2.0 fusion.18
  526.6 2.6 fusion.37
  531.6 2.3 copy.725
  536.3 2.2 collective-permute-start.4
  541.1 1.9 select_n.220
  543.0 1.9 select_n.223
  545.7 2.6 copy.727
  551.1 1.9 collective-permute-start.6
  553.0 3.9 collective-permute-start.7
  559.2 266.2 %all-reduce.5.cloned.1.call-done = bf16[16,12,4,128]{1,0,3,2:T(8,128)(2,1)} async-done(((bf16[16,12,4,128]{1,0,3,2:T(8,128)(2,1)}), bf16[16,12,4,128]{1,0,3,2:T(8,128)(2,1)}) %all-reduce.5.cloned.1.call-update) | async-done | bytes 196624 | tf_op jit(solution)/shard_map/psum | solution.py:75
  825.4 3.0 copy.731
  837.1 3.8 scatter.36
  844.2 18.6 %scatter.39 = bf16[16,12,18,34]{3,0,2,1:T(8,128)(2,1)S(1)} dynamic-update-slice(bf16[16,12,18,34]{3,0,2,1:T(8,128)(2,1)S(1)} %scatter.36, bf16[16,12,18,1]{3,0,2,1:T(8,128)(2,1)S(1)} %copy.735, s32[]{:T(128)} %constant.235.clone.1, s32[]{:T(128)} %constant.235.clone.1, s32[]{:T(128)} %constant.235.clone.1, s32[]{:T(128)} %constant.249.clone.1) | dynamic-update-slice | bytes 13828 | tf_op jit(solution)/shard_map/scatter | solution.py:97
  865.5 162.9 %all-gather.5.cloned.1.call-done = bf16[128,12,18,34]{3,0,2,1:T(8,128)(2,1)} async-done(((bf16[16,12,18,34]{3,0,2,1:T(8,128)(2,1)}), bf16[128,12,18,34]{3,0,2,1:T(8,128)(2,1)}) %all-gather.5.cloned.1.call-update) | async-done | bytes 1880080 | tf_op jit(solution)/shard_map/all_gather | solution.py:158
  1028.4 4.8 fusion.2
  1034.3 1.9 fusion.10
  1037.2 1.9 fusion.14
  1040.9 1.9 fusion.8
  1044.1 2.3 add_convert_fusion
  (201 shorter events, 80.0 us)
Async XLA Ops:
  7.2 503.6 %copy-start = (bf16[3,3,128,128]{3,2,1,0:T(8,128)(2,1)S(1)}, bf16[3,3,128,128]{3,2,1,0:T(8,128)(2,1)}, u32[]{:S(2)}) copy-start(bf16[3,3,128,128]{3,2,1,0:T(8,128)(2,1)} %param.27) | copy-start | bytes 884740
  7.2 300.8 %all-reduce.3.cloned.1.call-start = ((), (), s32[]{:S(2)}) async-start(), calls=%async_computation | async-start | bytes 4194304 | tf_op jit(solution)/shard_map/psum | solution.py:75
  25.7 10.9 %copy-start.17 = (s32[12,4,3]{0,1,2:T(4,128)S(1)}, s32[12,4,3]{0,1,2:T(4,128)}, u32[]{:S(2)}) copy-start(s32[12,4,3]{0,1,2:T(4,128)} %param.28) | copy-start | bytes 1732
  25.7 12.0 %copy-start.26 = (s32[12,4,2]{0,2,1:T(2,128)S(1)}, s32[12,4,2]{0,2,1:T(2,128)}, u32[]{:S(2)}) copy-start(s32[12,4,2]{0,2,1:T(2,128)} %param.29) | copy-start | bytes 1156
  25.7 485.0 %all-gather.3.cloned.1.call-start = ((), (), s32[]{:S(2)}) async-start(), calls=%async_computation.1 | async-start | bytes 7962624 | tf_op jit(solution)/shard_map/all_gather | solution.py:151
  27.0 12.3 %collective-permute-start = (bf16[16,12,16,1]{2,0,3,1:T(8,128)(2,1)S(1)}, bf16[16,12,16,1]{2,0,3,1:T(8,128)(2,1)S(1)}, u32[]{:S(2)}, u32[]{:S(2)}) collective-permute-start(bf16[16,12,16,1]{2,0,3,1:T(8,128)(2,1)S(1)} %copy.684), channel_id=1, source_target_pairs={{0,64},{64,128},{128,192},{1,65},{65,129},{129,193},{2,66},{66,130... | collective-permute-start | bytes 18440 | tf_op jit(solution)/shard_map/ppermute | solution.py:16
  35.3 6.0 collective-permute-start.1
  43.6 5.9 collective-permute-start.2
  45.5 5.4 collective-permute-start.3
  53.1 258.7 %copy-start.15 = (pred[12]{0:T(512)(128)(4,1)S(1)}, pred[12]{0:T(512)(128)(4,1)}, u32[]{:S(2)}) copy-start(pred[12]{0:T(512)(128)(4,1)} %get-tuple-element.166) | copy-start | bytes 40
  53.1 259.6 %copy-start.13 = (pred[12]{0:T(512)(128)(4,1)S(1)}, pred[12]{0:T(512)(128)(4,1)}, u32[]{:S(2)}) copy-start(pred[12]{0:T(512)(128)(4,1)} %get-tuple-element.164) | copy-start | bytes 40
  311.0 4.6 copy-start.20
  311.0 4.7 copy-start.11
  311.0 4.9 copy-start.22
  313.8 3.6 copy-start.24
  346.1 479.3 %all-reduce.5.cloned.1.call-start = ((), (), s32[]{:S(2)}) async-start(), calls=%async_computation.2 | async-start | bytes 4194304 | tf_op jit(solution)/shard_map/psum | solution.py:75
  510.7 4.8 copy-start.2
  535.1 9.9 copy-start.7
  535.1 10.2 copy-start.6
  536.3 12.1 %collective-permute-start.4 = (bf16[16,12,16,1]{2,0,3,1:T(8,128)(2,1)S(1)}, bf16[16,12,16,1]{2,0,3,1:T(8,128)(2,1)S(1)}, u32[]{:S(2)}, u32[]{:S(2)}) collective-permute-start(bf16[16,12,16,1]{2,0,3,1:T(8,128)(2,1)S(1)} %copy.720), channel_id=1, source_target_pairs={{0,64},{64,128},{128,192},{1,65},{65,129},{129,193},{2,66},{66,130... | collective-permute-start | bytes 18440 | tf_op jit(solution)/shard_map/ppermute | solution.py:16
  539.8 9.9 collective-permute-start.5
  548.4 480.1 %all-gather.5.cloned.1.call-start = ((), (), s32[]{:S(2)}) async-start(), calls=%async_computation.3 | async-start | bytes 7962624 | tf_op jit(solution)/shard_map/all_gather | solution.py:158
  551.1 5.8 collective-permute-start.6
  553.0 5.4 collective-permute-start.7
  559.1 272.2 %copy-start.16 = (pred[12]{0:T(512)(128)(4,1)S(1)}, pred[12]{0:T(512)(128)(4,1)}, u32[]{:S(2)}) copy-start(pred[12]{0:T(512)(128)(4,1)} %get-tuple-element.166) | copy-start | bytes 40
  559.2 272.4 %copy-start.25 = (pred[12]{0:T(512)(128)(4,1)S(1)}, pred[12]{0:T(512)(128)(4,1)}, u32[]{:S(2)}) copy-start(pred[12]{0:T(512)(128)(4,1)} %get-tuple-element.162) | copy-start | bytes 40
  559.2 272.5 %copy-start.14 = (pred[12]{0:T(512)(128)(4,1)S(1)}, pred[12]{0:T(512)(128)(4,1)}, u32[]{:S(2)}) copy-start(pred[12]{0:T(512)(128)(4,1)} %get-tuple-element.164) | copy-start | bytes 40
  559.2 272.7 %copy-start.23 = (pred[12]{0:T(512)(128)(4,1)S(1)}, pred[12]{0:T(512)(128)(4,1)}, u32[]{:S(2)}) copy-start(pred[12]{0:T(512)(128)(4,1)} %get-tuple-element.161) | copy-start | bytes 40
  828.4 5.5 copy-start.21
  828.5 5.6 copy-start.9
  842.9 20.9 %copy-start.5 = (bf16[16,12,16,32]{3,0,2,1:T(8,128)(2,1)S(1)}, bf16[16,12,16,32]{3,0,2,1:T(8,128)(2,1)}, u32[]{:S(2)}) copy-start(bf16[16,12,16,32]{3,0,2,1:T(8,128)(2,1)} %get-tuple-element.139) | copy-start | bytes 589828
  1028.4 4.8 copy-start.1
  (7 other events, 9.8 us)
Sparse Core Ops, SparseCore 0:
  25.8 282.0 all-reduce.2
  346.2 164.4 all-gather.2
  548.5 276.8 all-reduce.4
  863.9 164.4 all-gather.4
where the time goes:
time: 1060 us
  waiting for transfers between devices  850 us (80%)
  local copies, waits for them, and re-layouts  117 us (11%)
  matrix products  36.3 us (3%)
  starting transfers between devices  24 us (2%)
  between operations  15.2 us (1%)
  other arithmetic  12.9 us (1%)
    psum x2, waiting for transfers between devices, face_lines_of(): return lax.psum(contrib.astype(jnp.bfloat16), ('px', 'py'))  521 us
    all_gather x1, waiting for transfers between devices, local(): lax.all_gather(grad_pad, 'ch', axis=0, tiled=True)  163 us
    all_gather x1, waiting for transfers between devices, local(): lax.all_gather(feat_pad, 'ch', axis=0, tiled=True)  163 us
    scatter x2, local copies, waits for them, and re-layouts, pad_field(): padded.at[:, :, :, -1]  36.9 us
  transfers between devices with their start and end apart: 12, of which 7 were waited for; matrix products, arithmetic and copies ran while one was open for 2% of the time, Pallas kernels for 0%

commit v1 on v0

--- a/solution.py
+++ b/solution.py
@@ -72,7 +72,7 @@
         ],
         axis=2,
     )
-    return lax.psum(contrib.astype(jnp.bfloat16), ("px", "py"))
+    return jnp.sum(lax.all_gather(contrib.astype(jnp.bfloat16), ("px", "py")), axis=0)
 
 
 def pad_field(field, edge_table, corner_table):

time: 1060 us -> 626 us (0.59)
  waiting for transfers between devices: 850 us -> 410 us
    psum x2 -> x0, waiting for transfers between devices: 521 us -> none  [face_lines_of(): return lax.psum(contrib.astype(jnp.bfloat16), ('px', 'py'))]
    all_gather x0 -> x2, waiting for transfers between devices: none -> 86.3 us  [face_lines_of(): lax.all_gather(contrib.astype(jnp.bfloat16), ('px', 'py'))]
  transfers between devices with their start and end apart: 12 -> 12, of which waited for: 7 -> 10; matrix products, arithmetic and copies ran while one was open for 2% -> 3% of each run, Pallas kernels for 0% -> 0%
where the time goes in v1:
time: 626 us; the launch traced here: 618 us
  waiting for transfers between devices  410 us (65%)
  local copies, waits for them, and re-layouts  107 us (17%)
  matrix products  36.3 us (6%)
  starting transfers between devices  27.2 us (4%)
  other arithmetic  22.8 us (4%)
  between operations  15.2 us (2%)
    all_gather x1, waiting for transfers between devices, local(): lax.all_gather(grad_pad, 'ch', axis=0, tiled=True)  158 us
    all_gather x1, waiting for transfers between devices, local(): lax.all_gather(feat_pad, 'ch', axis=0, tiled=True)  158 us
    all_gather x2, waiting for transfers between devices, face_lines_of(): lax.all_gather(contrib.astype(jnp.bfloat16), ('px', 'py'))  86.3 us
    scatter x2, local copies, waits for them, and re-layouts, pad_field(): padded.at[:, :, :, -1]  36.9 us
    select_n x12, local copies, waits for them, and re-layouts, placed(): jnp.where(active, lax.dynamic_update_slice_in_dim(blank, values.astype(jn...  20.3 us
    dot_general x9, matrix products, forward_taps(): jnp.einsum('oc,cfab->ofab', taps[tap_row, tap_col], window, preferred_ele...  18.4 us
    dot_general x9, matrix products, backward_taps(): jnp.einsum('oc,ofab->cfab', taps[tap_row, tap_col], window, preferred_ele...  17.9 us
    ppermute x4, starting transfers between devices, with_halo(): before = lax.ppermute(last, axis, up)  16.4 us
  transfers between devices with their start and end apart: 12, of which 10 were waited for; matrix products, arithmetic and copies ran while one was open for 3% of the time, Pallas kernels for 0%

profile of v1, /device:TPU:8, one launch (start us, length us, event | category | flops | bytes accessed | tf_op | source)
XLA Modules:
  0.0 618.4 jit_solution(6113563107516248471)
XLA Ops:
  11.2 3.0 copy.926
  16.1 2.7 select_n.206
  18.8 2.7 select_n.210
  25.0 7.1 %collective-permute-start = (bf16[16,12,16,1]{2,0,3,1:T(8,128)(2,1)S(1)}, bf16[16,12,16,1]{2,0,3,1:T(8,128)(2,1)S(1)}, u32[]{:S(2)}, u32[]{:S(2)}) collective-permute-start(bf16[16,12,16,1]{2,0,3,1:T(8,128)(2,1)S(1)} %copy.912), channel_id=1, source_target_pairs={{0,64},{64,128},{128,192},{1,65},{65,129},{129,193},{2,66},{66,130... | collective-permute-start | bytes 18440 | tf_op jit(solution)/shard_map/ppermute | solution.py:16
  41.6 1.9 collective-permute-start.2
  43.6 3.9 collective-permute-start.3
  51.5 44.8 %all-gather.5.cloned.1.call-done = bf16[32,16,12,4,128]{4,1,3,2,0:T(8,128)(2,1)} async-done(((bf16[1,16,12,4,128]{4,1,3,2,0:T(8,128)(2,1)}), bf16[32,16,12,4,128]{4,1,3,2,0:T(8,128)(2,1)}) %all-gather.5.cloned.1.call-update) | async-done | bytes 6291472 | tf_op jit(solution)/shard_map/all_gather | solution.py:75
  96.3 4.3 reduce_sum.24
  108.7 3.8 scatter.30
  116.5 18.3 %scatter.31 = bf16[16,12,18,34]{3,0,2,1:T(8,128)(2,1)S(1)} dynamic-update-slice(bf16[16,12,18,34]{3,0,2,1:T(8,128)(2,1)S(1)} %scatter.30, bf16[16,12,18,1]{3,0,2,1:T(8,128)(2,1)S(1)} %copy.941, s32[]{:T(128)} %constant.293.clone.1, s32[]{:T(128)} %constant.293.clone.1, s32[]{:T(128)} %constant.293.clone.1, s32[]{:T(128)} %constant.308.clone.1) | dynamic-update-slice | bytes 13828 | tf_op jit(solution)/shard_map/scatter | solution.py:97
  137.7 157.8 %all-gather.7.cloned.1.call-done = bf16[128,12,18,34]{3,0,2,1:T(8,128)(2,1)} async-done(((bf16[16,12,18,34]{3,0,2,1:T(8,128)(2,1)}), bf16[128,12,18,34]{3,0,2,1:T(8,128)(2,1)}) %all-gather.7.cloned.1.call-update) | async-done | bytes 1880080 | tf_op jit(solution)/shard_map/all_gather | solution.py:151
  295.5 4.7 fusion.20
  309.5 2.0 fusion.18
  311.4 2.6 fusion.37
  316.3 2.3 copy.961
  319.9 1.9 select_n.232
  321.9 1.9 select_n.235
  328.0 5.4 collective-permute-start.4
  337.2 3.4 collective-permute-done.5
  342.0 1.9 collective-permute-start.6
  343.9 3.9 collective-permute-start.7
  350.5 41.5 %all-gather.9.cloned.1.call-done = bf16[32,16,12,4,128]{4,1,3,2,0:T(8,128)(2,1)} async-done(((bf16[1,16,12,4,128]{4,1,3,2,0:T(8,128)(2,1)}), bf16[32,16,12,4,128]{4,1,3,2,0:T(8,128)(2,1)}) %all-gather.9.cloned.1.call-update) | async-done | bytes 6291472 | tf_op jit(solution)/shard_map/all_gather | solution.py:75
  392.0 4.3 reduce_sum.25
  405.1 3.8 scatter.36
  412.2 18.6 %scatter.39 = bf16[16,12,18,34]{3,0,2,1:T(8,128)(2,1)S(1)} dynamic-update-slice(bf16[16,12,18,34]{3,0,2,1:T(8,128)(2,1)S(1)} %scatter.36, bf16[16,12,18,1]{3,0,2,1:T(8,128)(2,1)S(1)} %copy.975, s32[]{:T(128)} %constant.293.clone.1, s32[]{:T(128)} %constant.293.clone.1, s32[]{:T(128)} %constant.293.clone.1, s32[]{:T(128)} %constant.308.clone.1) | dynamic-update-slice | bytes 13828 | tf_op jit(solution)/shard_map/scatter | solution.py:97
  433.5 158.3 %all-gather.11.cloned.1.call-done = bf16[128,12,18,34]{3,0,2,1:T(8,128)(2,1)} async-done(((bf16[16,12,18,34]{3,0,2,1:T(8,128)(2,1)}), bf16[128,12,18,34]{3,0,2,1:T(8,128)(2,1)}) %all-gather.11.cloned.1.call-update) | async-done | bytes 1880080 | tf_op jit(solution)/shard_map/all_gather | solution.py:158
  591.8 4.8 fusion.2
  597.7 1.9 fusion.10
  600.6 1.9 fusion.14
  602.4 1.9 fusion.4
  604.3 1.9 fusion.8
  607.5 2.3 add_convert_fusion
  (203 shorter events, 81.9 us)
Async XLA Ops:
  7.2 288.4 %copy-start = (bf16[3,3,128,128]{3,2,1,0:T(8,128)(2,1)S(1)}, bf16[3,3,128,128]{3,2,1,0:T(8,128)(2,1)}, u32[]{:S(2)}) copy-start(bf16[3,3,128,128]{3,2,1,0:T(8,128)(2,1)} %param.27) | copy-start | bytes 884740
  7.2 89.2 %all-gather.5.cloned.1.call-start = ((), (), s32[]{:S(2)}) async-start(), calls=%async_computation | async-start | bytes 6488064 | tf_op jit(solution)/shard_map/all_gather | solution.py:75
  16.0 18.6 %copy-start.15 = (s32[12,4,3]{0,1,2:T(4,128)S(1)}, s32[12,4,3]{0,1,2:T(4,128)}, u32[]{:S(2)}) copy-start(s32[12,4,3]{0,1,2:T(4,128)} %param.28) | copy-start | bytes 1732
  16.0 19.8 %copy-start.24 = (s32[12,4,2]{0,2,1:T(2,128)S(1)}, s32[12,4,2]{0,2,1:T(2,128)}, u32[]{:S(2)}) copy-start(s32[12,4,2]{0,2,1:T(2,128)} %param.29) | copy-start | bytes 1156
  23.8 271.8 %all-gather.7.cloned.1.call-start = ((), (), s32[]{:S(2)}) async-start(), calls=%async_computation.1 | async-start | bytes 7962624 | tf_op jit(solution)/shard_map/all_gather | solution.py:151
  25.0 12.4 %collective-permute-start = (bf16[16,12,16,1]{2,0,3,1:T(8,128)(2,1)S(1)}, bf16[16,12,16,1]{2,0,3,1:T(8,128)(2,1)S(1)}, u32[]{:S(2)}, u32[]{:S(2)}) collective-permute-start(bf16[16,12,16,1]{2,0,3,1:T(8,128)(2,1)S(1)} %copy.912), channel_id=1, source_target_pairs={{0,64},{64,128},{128,192},{1,65},{65,129},{129,193},{2,66},{66,130... | collective-permute-start | bytes 18440 | tf_op jit(solution)/shard_map/ppermute | solution.py:16
  33.3 6.0 collective-permute-start.1
  41.6 6.4 %collective-permute-start.2 = (bf16[16,12,1,34]{3,0,1,2:T(8,128)(2,1)S(1)}, bf16[16,12,1,34]{3,0,1,2:T(8,128)(2,1)S(1)}, u32[]{:S(2)}, u32[]{:S(2)}) collective-permute-start(bf16[16,12,1,34]{3,0,1,2:T(8,128)(2,1)S(1)} %get-tuple-element.146), channel_id=1, source_target_pairs={{0,8},{8,16},{16,24},{24,32},{32,40},{40,48},{48,56},{1,9},{9,17},... | collective-permute-start | bytes 39176 | tf_op jit(solution)/shard_map/ppermute | solution.py:16
  43.6 5.7 collective-permute-start.3
  51.5 50.0 %copy-start.13 = (pred[12]{0:T(512)(128)(4,1)S(1)}, pred[12]{0:T(512)(128)(4,1)}, u32[]{:S(2)}) copy-start(pred[12]{0:T(512)(128)(4,1)} %get-tuple-element.172) | copy-start | bytes 40
  51.5 50.9 %copy-start.11 = (pred[12]{0:T(512)(128)(4,1)S(1)}, pred[12]{0:T(512)(128)(4,1)}, u32[]{:S(2)}) copy-start(pred[12]{0:T(512)(128)(4,1)} %get-tuple-element.170) | copy-start | bytes 40
  100.6 4.7 copy-start.18
  100.6 4.8 copy-start.9
  100.7 5.0 copy-start.20
  103.6 3.6 copy-start.22
  112.5 2.5 copy-start.16
  135.9 256.1 %all-gather.9.cloned.1.call-start = ((), (), s32[]{:S(2)}) async-start(), calls=%async_computation.2 | async-start | bytes 6488064 | tf_op jit(solution)/shard_map/all_gather | solution.py:75
  295.5 4.8 copy-start.2
  326.7 265.1 %all-gather.11.cloned.1.call-start = ((), (), s32[]{:S(2)}) async-start(), calls=%async_computation.3 | async-start | bytes 7962624 | tf_op jit(solution)/shard_map/all_gather | solution.py:158
  328.0 8.0 %collective-permute-start.4 = (bf16[16,12,16,1]{2,0,3,1:T(8,128)(2,1)S(1)}, bf16[16,12,16,1]{2,0,3,1:T(8,128)(2,1)S(1)}, u32[]{:S(2)}, u32[]{:S(2)}) collective-permute-start(bf16[16,12,16,1]{2,0,3,1:T(8,128)(2,1)S(1)} %copy.954), channel_id=1, source_target_pairs={{0,64},{64,128},{128,192},{1,65},{65,129},{129,193},{2,66},{66,130... | collective-permute-start | bytes 18440 | tf_op jit(solution)/shard_map/ppermute | solution.py:16
  334.6 6.0 collective-permute-start.5
  342.0 6.2 %collective-permute-start.6 = (bf16[16,12,1,34]{3,0,2,1:T(8,128)(2,1)S(1)}, bf16[16,12,1,34]{3,0,2,1:T(8,128)(2,1)S(1)}, u32[]{:S(2)}, u32[]{:S(2)}) collective-permute-start(bf16[16,12,1,34]{3,0,2,1:T(8,128)(2,1)S(1)} %get-tuple-element.134), channel_id=1, source_target_pairs={{0,8},{8,16},{16,24},{24,32},{32,40},{40,48},{48,56},{1,9},{9,17},... | collective-permute-start | bytes 39176 | tf_op jit(solution)/shard_map/ppermute | solution.py:16
  343.9 5.8 collective-permute-start.7
  350.5 48.7 %copy-start.14 = (pred[12]{0:T(512)(128)(4,1)S(1)}, pred[12]{0:T(512)(128)(4,1)}, u32[]{:S(2)}) copy-start(pred[12]{0:T(512)(128)(4,1)} %get-tuple-element.172) | copy-start | bytes 40
  350.5 48.9 %copy-start.23 = (pred[12]{0:T(512)(128)(4,1)S(1)}, pred[12]{0:T(512)(128)(4,1)}, u32[]{:S(2)}) copy-start(pred[12]{0:T(512)(128)(4,1)} %get-tuple-element.168) | copy-start | bytes 40
  350.5 49.0 %copy-start.12 = (pred[12]{0:T(512)(128)(4,1)S(1)}, pred[12]{0:T(512)(128)(4,1)}, u32[]{:S(2)}) copy-start(pred[12]{0:T(512)(128)(4,1)} %get-tuple-element.170) | copy-start | bytes 40
  350.5 49.2 %copy-start.21 = (pred[12]{0:T(512)(128)(4,1)S(1)}, pred[12]{0:T(512)(128)(4,1)}, u32[]{:S(2)}) copy-start(pred[12]{0:T(512)(128)(4,1)} %get-tuple-element.167) | copy-start | bytes 40
  397.0 4.9 copy-start.19
  397.7 4.3 copy-start.7
  408.9 1.8 copy-start.17
  410.9 20.9 %copy-start.5 = (bf16[16,12,16,32]{3,0,2,1:T(8,128)(2,1)S(1)}, bf16[16,12,16,32]{3,0,2,1:T(8,128)(2,1)}, u32[]{:S(2)}) copy-start(bf16[16,12,16,32]{3,0,2,1:T(8,128)(2,1)} %get-tuple-element.137) | copy-start | bytes 589828
  591.8 4.8 copy-start.1
  (5 other events, 5.4 us)
Sparse Core Ops, SparseCore 0:
  23.9 72.4 all-gather.4
  136.0 159.4 all-gather.6
  326.8 65.1 all-gather.8
  431.9 159.8 all-gather.10
